TPU v7x, 256 devices: a whole 4x4x8 slice. The times are simulated.
256 devices in a mesh: tm: 64 (over x, z_lo, y), space: 4 (over z_hi, core).
Axes of the slice: x: 4, y: 4, z: 8 (z_hi: 2, z_lo: 4; z = z_hi * 4 + z_lo), core: 2. Of those that a mesh axis runs over, the one named last changes fastest.
Arguments:
- start: float32 [64, 2, 32, 64, 128], P('tm', None, 'space'), may hold values from -0.2 to 1.2
- conduct: float32 [32, 64, 128], P('space'), may hold values from 0.03 to 0.12
- threshold: float32 [32, 64, 128], P('space'), may hold values from 0.05 to 0.45
- recovery: float32 [32, 64, 128], P('space'), may hold values from 0.02 to 0.3
Outputs:
- final: float32 [64, 2, 32, 64, 128], P('tm', None, 'space')
All inputs are finite; a program needn't handle non-finite values.
Results may differ from a plain program's by a relative error of at most 0.0001.
Values sent between devices are 32-bit elements; how exact they have to be, the bound alone decides.
No kernel may reach another device: no remote copies, remote signals or barrier semaphores. Data moves between devices by JAX's collectives and lax.ppermute only.
A program may use at most 64 MiB of HBM per device.

v0:
```python
import jax
import jax.numpy as jnp
from jax import lax
from jax.sharding import PartitionSpec as P

ITERS = 2


quad_first = (5.0 / 24.0, 1.0 / 3.0, -1.0 / 24.0)
quad_second = (-1.0 / 24.0, 1.0 / 3.0, 5.0 / 24.0)
node_step = 0.5
reaction = 2.0
recovery_ratio = 0.5


def extended(cells, sides, width):
    for axis, dim in sides:
        count = lax.axis_size(axis)
        ends = count - 1
        head = lax.slice_in_dim(cells, 0, width, axis=dim)
        tail = lax.slice_in_dim(cells, cells.shape[dim] - width, cells.shape[dim], axis=dim)
        cells = jnp.concatenate(
            [
                lax.ppermute(tail, axis, [(i, (i + 1) % count) for i in range(ends)]),
                cells,
                lax.ppermute(head, axis, [((i + 1) % count, i) for i in range(ends)]),
            ],
            axis=dim,
        )
    return cells


def passed_along(array, axis, by):
    count = lax.axis_size(axis)
    pairs = [(i, i + by) for i in range(count) if 0 <= i + by < count]
    return lax.ppermute(array, axis, pairs)


def quadrature(weights, terms):
    return weights[0] * terms[0] + weights[1] * terms[1] + weights[2] * terms[2]


def fine_laplace(padded, values):
    summed = padded[:, 2:, 1:-1, 1:-1] + padded[:, :-2, 1:-1, 1:-1]
    summed = summed + padded[:, 1:-1, 2:, 1:-1] + padded[:, 1:-1, :-2, 1:-1]
    summed = summed + padded[:, 1:-1, 1:-1, 2:] + padded[:, 1:-1, 1:-1, :-2]
    return summed - 6.0 * values


def coarse_laplace(padded, values):
    along_x = padded[:, 2:, 1:-1, 1:-1] + padded[:, :-2, 1:-1, 1:-1] - 2.0 * values
    along_y = padded[:, 1:-1, 2:, 1:-1] + padded[:, 1:-1, :-2, 1:-1] - 2.0 * values
    along_z = padded[:, 1:-1, 1:-1, 2:] + padded[:, 1:-1, 1:-1, :-2] - 2.0 * values
    return 0.25 * along_x + 0.25 * along_y + along_z


def forces(states, laplace, coeffs):
    conduct, threshold, recovery = coeffs
    excite = states[:, 0]
    slower = states[:, 1]
    driving = conduct * laplace + reaction * excite * (1.0 - excite) * (excite - threshold) - slower
    relaxing = recovery * (excite - recovery_ratio * slower)
    return jnp.stack([driving, relaxing], axis=1)


def restrict(values):
    sizes_of = values.shape
    blocks = values.reshape(
        sizes_of[:-3] + (sizes_of[-3] // 2, 2, sizes_of[-2] // 2, 2, sizes_of[-1])
    )
    return 0.25 * jnp.sum(blocks, axis=(-4, -2))


def prolong(values):
    sizes_of = values.shape
    widened = jnp.broadcast_to(
        values[..., :, None, :, None, :],
        sizes_of[:-3] + (sizes_of[-3], 2, sizes_of[-2], 2, sizes_of[-1]),
    )
    return widened.reshape(sizes_of[:-3] + (2 * sizes_of[-3], 2 * sizes_of[-2], sizes_of[-1]))


def side_pad(padded_x):
    return jnp.pad(padded_x, ((0, 0), (0, 0), (1, 1), (1, 1)))


def fine_single(state, coeffs):
    stacked = state[None]
    padded_x = extended(stacked[:, 0], (("space", 1),), 1)
    return forces(stacked, fine_laplace(side_pad(padded_x), stacked[:, 0]), coeffs)[0]


def per_device(start, conduct, threshold, recovery):
    fine_coeffs = (conduct, threshold, recovery)
    coarse_coeffs = (restrict(conduct), restrict(threshold), restrict(recovery))
    initial = start[0]
    start_terms = fine_single(initial, fine_coeffs)
    upper_nodes = jnp.stack([initial, initial])
    upper_terms = jnp.stack([start_terms, start_terms])
    old_first_terms = start_terms
    is_head = lax.axis_index("tm") == 0
    result = initial
    for sweep_index in range(ITERS):
        final_pass = sweep_index + 1 == ITERS
        if sweep_index == 0:
            term_zero = start_terms
        else:
            padded_x = extended(upper_nodes[:, 0], (("space", 1),), 1)
            upper_terms = forces(
                upper_nodes, fine_laplace(side_pad(padded_x), upper_nodes[:, 0]), fine_coeffs
            )
            term_zero = fine_single(initial, fine_coeffs)
        old_terms = (old_first_terms, upper_terms[0], upper_terms[1])
        node_one = (
            initial + node_step * (term_zero - old_terms[0]) + quadrature(quad_first, old_terms)
        )
        term_one = fine_single(node_one, fine_coeffs)
        node_two = (
            node_one + node_step * (term_one - old_terms[1]) + quadrature(quad_second, old_terms)
        )
        term_two = fine_single(node_two, fine_coeffs)
        new_terms = (term_zero, term_one, term_two)
        sum_first = quadrature(quad_first, new_terms)
        sum_second = quadrature(quad_second, new_terms)
        coarse_zero = restrict(initial)
        base_one = restrict(node_one)
        coarse_one = coarse_zero + restrict(sum_first)
        pair_states = jnp.stack([base_one, coarse_one])
        coarse_x = extended(pair_states[:, 0], (("space", 1),), 1)
        pair_terms = forces(
            pair_states, coarse_laplace(side_pad(coarse_x), pair_states[:, 0]), coarse_coeffs
        )
        coarse_two = coarse_one + node_step * (pair_terms[1] - pair_terms[0]) + restrict(sum_second)
        coarse_jump = coarse_two - restrict(node_two)
        node_two_new = node_two + prolong(coarse_jump)
        if final_pass:
            result = node_two_new
        else:
            node_one_new = node_one + prolong(coarse_one - base_one)
            received = passed_along(node_two_new, "tm", 1)
            upper_nodes = jnp.stack([node_one_new, node_two_new])
            old_first_terms = term_zero
            initial = jnp.where(is_head, start[0], received)
    return result[None]


def solution(mesh):
    placed = (
        P("tm", None, "space", None, None),
        P("space", None, None),
        P("space", None, None),
        P("space", None, None),
    )
    return jax.shard_map(
        per_device,
        mesh=mesh,
        in_specs=placed,
        out_specs=P("tm", None, "space", None, None),
        check_vma=False,
    )
```

profile of v0, /device:TPU:7, one launch (start us, length us, event | category | flops | bytes accessed | tf_op | source)
XLA Modules:
  0.0 132.5 jit_solution(16184439660468529342)
XLA Ops:
  0.0 1.1 slice_bitcast_fusion.5
  1.1 2.6 %collective-permute-start = (f32[1,1,64,128]{3,2,1,0:T(8,128)S(1)}, f32[1,1,64,128]{3,2,1,0:T(8,128)S(1)}, u32[]{:S(2)}, u32[]{:S(2)}) collective-permute-start(f32[1,1,64,128]{3,2,1,0:T(8,128)S(1)} %get-tuple-element.32), channel_id=1, source_target_pairs={{1,0},{2,1},{3,2},{5,4},{6,5},{7,6},{9,8},{10,9},{11,10},{13,12},{... | collective-permute-start | bytes 98312 | tf_op jit(solution)/shard_map/ppermute | solution.py:26
  3.7 8.7 %collective-permute-start.1 = (f32[1,1,64,128]{3,2,1,0:T(8,128)S(1)}, f32[1,1,64,128]{3,2,1,0:T(8,128)S(1)}, u32[]{:S(2)}, u32[]{:S(2)}) collective-permute-start(f32[1,1,64,128]{3,2,1,0:T(8,128)S(1)} %get-tuple-element.31), channel_id=1, source_target_pairs={{0,1},{1,2},{2,3},{4,5},{5,6},{6,7},{8,9},{9,10},{10,11},{12,13},{... | collective-permute-start | bytes 98312 | tf_op jit(solution)/shard_map/ppermute | solution.py:24
  12.4 1.2 fusion.80
  15.5 1.9 %collective-permute-start.2 = (f32[1,1,64,128]{3,2,1,0:T(8,128)S(1)}, f32[1,1,64,128]{3,2,1,0:T(8,128)S(1)}, u32[]{:S(2)}, u32[]{:S(2)}) collective-permute-start(f32[1,1,64,128]{3,2,1,0:T(8,128)S(1)} %get-tuple-element.30), channel_id=1, source_target_pairs={{1,0},{2,1},{3,2},{5,4},{6,5},{7,6},{9,8},{10,9},{11,10},{13,12},{... | collective-permute-start | bytes 98312 | tf_op jit(solution)/shard_map/ppermute | solution.py:26
  17.4 7.5 %collective-permute-start.3 = (f32[1,1,64,128]{3,2,1,0:T(8,128)S(1)}, f32[1,1,64,128]{3,2,1,0:T(8,128)S(1)}, u32[]{:S(2)}, u32[]{:S(2)}) collective-permute-start(f32[1,1,64,128]{3,2,1,0:T(8,128)S(1)} %get-tuple-element.29), channel_id=1, source_target_pairs={{0,1},{1,2},{2,3},{4,5},{5,6},{6,7},{8,9},{9,10},{10,11},{12,13},{... | collective-permute-start | bytes 98312 | tf_op jit(solution)/shard_map/ppermute | solution.py:24
  27.0 1.9 %collective-permute-start.4 = (f32[1,1,64,128]{3,2,1,0:T(8,128)S(1)}, f32[1,1,64,128]{3,2,1,0:T(8,128)S(1)}, u32[]{:S(2)}, u32[]{:S(2)}) collective-permute-start(f32[1,1,64,128]{3,2,1,0:T(8,128)S(1)} %get-tuple-element.28), channel_id=1, source_target_pairs={{1,0},{2,1},{3,2},{5,4},{6,5},{7,6},{9,8},{10,9},{11,10},{13,12},{... | collective-permute-start | bytes 98312 | tf_op jit(solution)/shard_map/ppermute | solution.py:26
  28.9 8.1 %collective-permute-start.5 = (f32[1,1,64,128]{3,2,1,0:T(8,128)S(1)}, f32[1,1,64,128]{3,2,1,0:T(8,128)S(1)}, u32[]{:S(2)}, u32[]{:S(2)}) collective-permute-start(f32[1,1,64,128]{3,2,1,0:T(8,128)S(1)} %get-tuple-element.27), channel_id=1, source_target_pairs={{0,1},{1,2},{2,3},{4,5},{5,6},{6,7},{8,9},{9,10},{10,11},{12,13},{... | collective-permute-start | bytes 98312 | tf_op jit(solution)/shard_map/ppermute | solution.py:24
  39.3 1.9 %collective-permute-start.6 = (f32[2,1,32,128]{3,2,1,0:T(8,128)S(1)}, f32[2,1,32,128]{3,2,1,0:T(8,128)S(1)}, u32[]{:S(2)}, u32[]{:S(2)}) collective-permute-start(f32[2,1,32,128]{3,2,1,0:T(8,128)S(1)} %get-tuple-element.36), channel_id=1, source_target_pairs={{1,0},{2,1},{3,2},{5,4},{6,5},{7,6},{9,8},{10,9},{11,10},{13,12},{... | collective-permute-start | bytes 98312 | tf_op jit(solution)/shard_map/ppermute | solution.py:26
  41.2 8.1 %collective-permute-start.7 = (f32[2,1,32,128]{3,2,1,0:T(8,128)S(1)}, f32[2,1,32,128]{3,2,1,0:T(8,128)S(1)}, u32[]{:S(2)}, u32[]{:S(2)}) collective-permute-start(f32[2,1,32,128]{3,2,1,0:T(8,128)S(1)} %get-tuple-element.35), channel_id=1, source_target_pairs={{0,1},{1,2},{2,3},{4,5},{5,6},{6,7},{8,9},{9,10},{10,11},{12,13},{... | collective-permute-start | bytes 98312 | tf_op jit(solution)/shard_map/ppermute | solution.py:24
  53.4 1.9 %collective-permute-start.11 = (f32[2,1,64,128]{3,2,1,0:T(8,128)}, f32[2,1,64,128]{3,2,1,0:T(8,128)S(1)}, u32[]{:S(2)}, u32[]{:S(2)}) collective-permute-start(f32[2,1,64,128]{3,2,1,0:T(8,128)} %get-tuple-element.14), channel_id=1, source_target_pairs={{1,0},{2,1},{3,2},{5,4},{6,5},{7,6},{9,8},{10,9},{11,10},{13,12},{... | collective-permute-start | bytes 196616 | tf_op jit(solution)/shard_map/ppermute | solution.py:26
  55.3 8.1 %collective-permute-start.12 = (f32[2,1,64,128]{3,2,1,0:T(8,128)}, f32[2,1,64,128]{3,2,1,0:T(8,128)S(1)}, u32[]{:S(2)}, u32[]{:S(2)}) collective-permute-start(f32[2,1,64,128]{3,2,1,0:T(8,128)} %get-tuple-element.13), channel_id=1, source_target_pairs={{0,1},{1,2},{2,3},{4,5},{5,6},{6,7},{8,9},{9,10},{10,11},{12,13},{... | collective-permute-start | bytes 196616 | tf_op jit(solution)/shard_map/ppermute | solution.py:24
  63.5 1.1 fusion.24
  64.5 3.2 %collective-permute-start.8 = (f32[2,8,64,128]{3,2,1,0:T(8,128)}, f32[2,8,64,128]{3,2,1,0:T(8,128)}, u32[]{:S(2)}, u32[]{:S(2)}) collective-permute-start(f32[2,8,64,128]{3,2,1,0:T(8,128)} %fusion.24), channel_id=1, source_target_pairs={{0,4},{4,8},{8,12},{12,16},{16,20},{20,24},{24,28},{28,32},{32,36}... | collective-permute-start | bytes 1572872 | tf_op jit(solution)/shard_map/ppermute | solution.py:36
  69.4 11.3 %collective-permute-done.8 = f32[2,8,64,128]{3,2,1,0:T(8,128)} collective-permute-done((f32[2,8,64,128]{3,2,1,0:T(8,128)}, f32[2,8,64,128]{3,2,1,0:T(8,128)}, u32[]{:S(2)}, u32[]{:S(2)}) %collective-permute-start.8) | collective-permute-done | bytes 524320 | tf_op jit(solution)/shard_map/ppermute | solution.py:36
  80.7 1.1 bitcast_select_fusion
  81.9 1.9 %collective-permute-start.9 = (f32[1,1,64,128]{3,2,1,0:T(8,128)S(1)}, f32[1,1,64,128]{3,2,1,0:T(8,128)S(1)}, u32[]{:S(2)}, u32[]{:S(2)}) collective-permute-start(f32[1,1,64,128]{3,2,1,0:T(8,128)S(1)} %get-tuple-element.24), channel_id=1, source_target_pairs={{1,0},{2,1},{3,2},{5,4},{6,5},{7,6},{9,8},{10,9},{11,10},{13,12},{... | collective-permute-start | bytes 98312 | tf_op jit(solution)/shard_map/ppermute | solution.py:26
  83.8 7.5 %collective-permute-start.10 = (f32[1,1,64,128]{3,2,1,0:T(8,128)S(1)}, f32[1,1,64,128]{3,2,1,0:T(8,128)S(1)}, u32[]{:S(2)}, u32[]{:S(2)}) collective-permute-start(f32[1,1,64,128]{3,2,1,0:T(8,128)S(1)} %get-tuple-element.23), channel_id=1, source_target_pairs={{0,1},{1,2},{2,3},{4,5},{5,6},{6,7},{8,9},{9,10},{10,11},{12,13},{... | collective-permute-start | bytes 98312 | tf_op jit(solution)/shard_map/ppermute | solution.py:24
  94.1 1.9 %collective-permute-start.13 = (f32[1,1,64,128]{3,2,1,0:T(8,128)S(1)}, f32[1,1,64,128]{3,2,1,0:T(8,128)S(1)}, u32[]{:S(2)}, u32[]{:S(2)}) collective-permute-start(f32[1,1,64,128]{3,2,1,0:T(8,128)S(1)} %get-tuple-element.20), channel_id=1, source_target_pairs={{1,0},{2,1},{3,2},{5,4},{6,5},{7,6},{9,8},{10,9},{11,10},{13,12},{... | collective-permute-start | bytes 98312 | tf_op jit(solution)/shard_map/ppermute | solution.py:26
  96.0 8.1 %collective-permute-start.14 = (f32[1,1,64,128]{3,2,1,0:T(8,128)S(1)}, f32[1,1,64,128]{3,2,1,0:T(8,128)S(1)}, u32[]{:S(2)}, u32[]{:S(2)}) collective-permute-start(f32[1,1,64,128]{3,2,1,0:T(8,128)S(1)} %get-tuple-element.19), channel_id=1, source_target_pairs={{0,1},{1,2},{2,3},{4,5},{5,6},{6,7},{8,9},{9,10},{10,11},{12,13},{... | collective-permute-start | bytes 98312 | tf_op jit(solution)/shard_map/ppermute | solution.py:24
  107.7 1.9 %collective-permute-start.15 = (f32[1,1,64,128]{3,2,1,0:T(8,128)S(1)}, f32[1,1,64,128]{3,2,1,0:T(8,128)S(1)}, u32[]{:S(2)}, u32[]{:S(2)}) collective-permute-start(f32[1,1,64,128]{3,2,1,0:T(8,128)S(1)} %get-tuple-element.18), channel_id=1, source_target_pairs={{1,0},{2,1},{3,2},{5,4},{6,5},{7,6},{9,8},{10,9},{11,10},{13,12},{... | collective-permute-start | bytes 98312 | tf_op jit(solution)/shard_map/ppermute | solution.py:26
  109.7 7.5 %collective-permute-start.16 = (f32[1,1,64,128]{3,2,1,0:T(8,128)S(1)}, f32[1,1,64,128]{3,2,1,0:T(8,128)S(1)}, u32[]{:S(2)}, u32[]{:S(2)}) collective-permute-start(f32[1,1,64,128]{3,2,1,0:T(8,128)S(1)} %get-tuple-element.17), channel_id=1, source_target_pairs={{0,1},{1,2},{2,3},{4,5},{5,6},{6,7},{8,9},{9,10},{10,11},{12,13},{... | collective-permute-start | bytes 98312 | tf_op jit(solution)/shard_map/ppermute | solution.py:24
  119.8 1.9 %collective-permute-start.17 = (f32[2,1,32,128]{3,2,1,0:T(8,128)S(1)}, f32[2,1,32,128]{3,2,1,0:T(8,128)S(1)}, u32[]{:S(2)}, u32[]{:S(2)}) collective-permute-start(f32[2,1,32,128]{3,2,1,0:T(8,128)S(1)} %get-tuple-element.34), channel_id=1, source_target_pairs={{1,0},{2,1},{3,2},{5,4},{6,5},{7,6},{9,8},{10,9},{11,10},{13,12},{... | collective-permute-start | bytes 98312 | tf_op jit(solution)/shard_map/ppermute | solution.py:26
  121.8 8.1 %collective-permute-start.18 = (f32[2,1,32,128]{3,2,1,0:T(8,128)S(1)}, f32[2,1,32,128]{3,2,1,0:T(8,128)S(1)}, u32[]{:S(2)}, u32[]{:S(2)}) collective-permute-start(f32[2,1,32,128]{3,2,1,0:T(8,128)S(1)} %get-tuple-element.33), channel_id=1, source_target_pairs={{0,1},{1,2},{2,3},{4,5},{5,6},{6,7},{8,9},{9,10},{10,11},{12,13},{... | collective-permute-start | bytes 98312 | tf_op jit(solution)/shard_map/ppermute | solution.py:24
  (134 shorter events, 22.6 us)
Async XLA Ops:
  0.0 13.8 %copy-start = (f32[1,2,8,64,128]{4,3,2,1,0:T(8,128)S(1)}, f32[1,2,8,64,128]{4,3,2,1,0:T(8,128)}, u32[]{:S(2)}) copy-start(f32[1,2,8,64,128]{4,3,2,1,0:T(8,128)} %param.4) | copy-start | bytes 1572868
  0.0 13.6 %copy-start.1 = (f32[8,64,128]{2,1,0:T(8,128)S(1)}, f32[8,64,128]{2,1,0:T(8,128)}, u32[]{:S(2)}) copy-start(f32[8,64,128]{2,1,0:T(8,128)} %param.7) | copy-start | bytes 786436
  0.0 14.2 %copy-start.2 = (f32[8,64,128]{2,1,0:T(8,128)S(1)}, f32[8,64,128]{2,1,0:T(8,128)}, u32[]{:S(2)}) copy-start(f32[8,64,128]{2,1,0:T(8,128)} %param.6) | copy-start | bytes 786436
  0.0 14.4 %copy-start.3 = (f32[8,64,128]{2,1,0:T(8,128)S(1)}, f32[8,64,128]{2,1,0:T(8,128)}, u32[]{:S(2)}) copy-start(f32[8,64,128]{2,1,0:T(8,128)} %param.5) | copy-start | bytes 786436
  1.1 13.5 %collective-permute-start = (f32[1,1,64,128]{3,2,1,0:T(8,128)S(1)}, f32[1,1,64,128]{3,2,1,0:T(8,128)S(1)}, u32[]{:S(2)}, u32[]{:S(2)}) collective-permute-start(f32[1,1,64,128]{3,2,1,0:T(8,128)S(1)} %get-tuple-element.32), channel_id=1, source_target_pairs={{1,0},{2,1},{3,2},{5,4},{6,5},{7,6},{9,8},{10,9},{11,10},{13,12},{... | collective-permute-start | bytes 98312 | tf_op jit(solution)/shard_map/ppermute | solution.py:26
  3.7 10.9 %collective-permute-start.1 = (f32[1,1,64,128]{3,2,1,0:T(8,128)S(1)}, f32[1,1,64,128]{3,2,1,0:T(8,128)S(1)}, u32[]{:S(2)}, u32[]{:S(2)}) collective-permute-start(f32[1,1,64,128]{3,2,1,0:T(8,128)S(1)} %get-tuple-element.31), channel_id=1, source_target_pairs={{0,1},{1,2},{2,3},{4,5},{5,6},{6,7},{8,9},{9,10},{10,11},{12,13},{... | collective-permute-start | bytes 98312 | tf_op jit(solution)/shard_map/ppermute | solution.py:24
  13.8 25.4 %copy-start.13 = (f32[4,32,128]{2,1,0:T(8,128)}, f32[4,32,128]{2,1,0:T(8,128)S(1)}, u32[]{:S(2)}) copy-start(f32[4,32,128]{2,1,0:T(8,128)S(1)} %broadcast_multiply_fusion) | copy-start | bytes 196612
  15.5 9.5 %collective-permute-start.2 = (f32[1,1,64,128]{3,2,1,0:T(8,128)S(1)}, f32[1,1,64,128]{3,2,1,0:T(8,128)S(1)}, u32[]{:S(2)}, u32[]{:S(2)}) collective-permute-start(f32[1,1,64,128]{3,2,1,0:T(8,128)S(1)} %get-tuple-element.30), channel_id=1, source_target_pairs={{1,0},{2,1},{3,2},{5,4},{6,5},{7,6},{9,8},{10,9},{11,10},{13,12},{... | collective-permute-start | bytes 98312 | tf_op jit(solution)/shard_map/ppermute | solution.py:26
  17.4 8.6 %collective-permute-start.3 = (f32[1,1,64,128]{3,2,1,0:T(8,128)S(1)}, f32[1,1,64,128]{3,2,1,0:T(8,128)S(1)}, u32[]{:S(2)}, u32[]{:S(2)}) collective-permute-start(f32[1,1,64,128]{3,2,1,0:T(8,128)S(1)} %get-tuple-element.29), channel_id=1, source_target_pairs={{0,1},{1,2},{2,3},{4,5},{5,6},{6,7},{8,9},{9,10},{10,11},{12,13},{... | collective-permute-start | bytes 98312 | tf_op jit(solution)/shard_map/ppermute | solution.py:24
  27.0 10.1 %collective-permute-start.4 = (f32[1,1,64,128]{3,2,1,0:T(8,128)S(1)}, f32[1,1,64,128]{3,2,1,0:T(8,128)S(1)}, u32[]{:S(2)}, u32[]{:S(2)}) collective-permute-start(f32[1,1,64,128]{3,2,1,0:T(8,128)S(1)} %get-tuple-element.28), channel_id=1, source_target_pairs={{1,0},{2,1},{3,2},{5,4},{6,5},{7,6},{9,8},{10,9},{11,10},{13,12},{... | collective-permute-start | bytes 98312 | tf_op jit(solution)/shard_map/ppermute | solution.py:26
  28.9 9.1 %collective-permute-start.5 = (f32[1,1,64,128]{3,2,1,0:T(8,128)S(1)}, f32[1,1,64,128]{3,2,1,0:T(8,128)S(1)}, u32[]{:S(2)}, u32[]{:S(2)}) collective-permute-start(f32[1,1,64,128]{3,2,1,0:T(8,128)S(1)} %get-tuple-element.27), channel_id=1, source_target_pairs={{0,1},{1,2},{2,3},{4,5},{5,6},{6,7},{8,9},{9,10},{10,11},{12,13},{... | collective-permute-start | bytes 98312 | tf_op jit(solution)/shard_map/ppermute | solution.py:24
  39.3 10.1 %collective-permute-start.6 = (f32[2,1,32,128]{3,2,1,0:T(8,128)S(1)}, f32[2,1,32,128]{3,2,1,0:T(8,128)S(1)}, u32[]{:S(2)}, u32[]{:S(2)}) collective-permute-start(f32[2,1,32,128]{3,2,1,0:T(8,128)S(1)} %get-tuple-element.36), channel_id=1, source_target_pairs={{1,0},{2,1},{3,2},{5,4},{6,5},{7,6},{9,8},{10,9},{11,10},{13,12},{... | collective-permute-start | bytes 98312 | tf_op jit(solution)/shard_map/ppermute | solution.py:26
  41.2 9.1 %collective-permute-start.7 = (f32[2,1,32,128]{3,2,1,0:T(8,128)S(1)}, f32[2,1,32,128]{3,2,1,0:T(8,128)S(1)}, u32[]{:S(2)}, u32[]{:S(2)}) collective-permute-start(f32[2,1,32,128]{3,2,1,0:T(8,128)S(1)} %get-tuple-element.35), channel_id=1, source_target_pairs={{0,1},{1,2},{2,3},{4,5},{5,6},{6,7},{8,9},{9,10},{10,11},{12,13},{... | collective-permute-start | bytes 98312 | tf_op jit(solution)/shard_map/ppermute | solution.py:24
  53.4 14.4 %collective-permute-start.11 = (f32[2,1,64,128]{3,2,1,0:T(8,128)}, f32[2,1,64,128]{3,2,1,0:T(8,128)S(1)}, u32[]{:S(2)}, u32[]{:S(2)}) collective-permute-start(f32[2,1,64,128]{3,2,1,0:T(8,128)} %get-tuple-element.14), channel_id=1, source_target_pairs={{1,0},{2,1},{3,2},{5,4},{6,5},{7,6},{9,8},{10,9},{11,10},{13,12},{... | collective-permute-start | bytes 196616 | tf_op jit(solution)/shard_map/ppermute | solution.py:26
  55.3 12.4 %collective-permute-start.12 = (f32[2,1,64,128]{3,2,1,0:T(8,128)}, f32[2,1,64,128]{3,2,1,0:T(8,128)S(1)}, u32[]{:S(2)}, u32[]{:S(2)}) collective-permute-start(f32[2,1,64,128]{3,2,1,0:T(8,128)} %get-tuple-element.13), channel_id=1, source_target_pairs={{0,1},{1,2},{2,3},{4,5},{5,6},{6,7},{8,9},{9,10},{10,11},{12,13},{... | collective-permute-start | bytes 196616 | tf_op jit(solution)/shard_map/ppermute | solution.py:24
  64.5 16.2 %collective-permute-start.8 = (f32[2,8,64,128]{3,2,1,0:T(8,128)}, f32[2,8,64,128]{3,2,1,0:T(8,128)}, u32[]{:S(2)}, u32[]{:S(2)}) collective-permute-start(f32[2,8,64,128]{3,2,1,0:T(8,128)} %fusion.24), channel_id=1, source_target_pairs={{0,4},{4,8},{8,12},{12,16},{16,20},{20,24},{24,28},{28,32},{32,36}... | collective-permute-start | bytes 1572872 | tf_op jit(solution)/shard_map/ppermute | solution.py:36
  81.9 9.9 %collective-permute-start.9 = (f32[1,1,64,128]{3,2,1,0:T(8,128)S(1)}, f32[1,1,64,128]{3,2,1,0:T(8,128)S(1)}, u32[]{:S(2)}, u32[]{:S(2)}) collective-permute-start(f32[1,1,64,128]{3,2,1,0:T(8,128)S(1)} %get-tuple-element.24), channel_id=1, source_target_pairs={{1,0},{2,1},{3,2},{5,4},{6,5},{7,6},{9,8},{10,9},{11,10},{13,12},{... | collective-permute-start | bytes 98312 | tf_op jit(solution)/shard_map/ppermute | solution.py:26
  83.8 8.6 %collective-permute-start.10 = (f32[1,1,64,128]{3,2,1,0:T(8,128)S(1)}, f32[1,1,64,128]{3,2,1,0:T(8,128)S(1)}, u32[]{:S(2)}, u32[]{:S(2)}) collective-permute-start(f32[1,1,64,128]{3,2,1,0:T(8,128)S(1)} %get-tuple-element.23), channel_id=1, source_target_pairs={{0,1},{1,2},{2,3},{4,5},{5,6},{6,7},{8,9},{9,10},{10,11},{12,13},{... | collective-permute-start | bytes 98312 | tf_op jit(solution)/shard_map/ppermute | solution.py:24
  94.1 12.0 %collective-permute-start.13 = (f32[1,1,64,128]{3,2,1,0:T(8,128)S(1)}, f32[1,1,64,128]{3,2,1,0:T(8,128)S(1)}, u32[]{:S(2)}, u32[]{:S(2)}) collective-permute-start(f32[1,1,64,128]{3,2,1,0:T(8,128)S(1)} %get-tuple-element.20), channel_id=1, source_target_pairs={{1,0},{2,1},{3,2},{5,4},{6,5},{7,6},{9,8},{10,9},{11,10},{13,12},{... | collective-permute-start | bytes 98312 | tf_op jit(solution)/shard_map/ppermute | solution.py:26
  96.0 10.1 %collective-permute-start.14 = (f32[1,1,64,128]{3,2,1,0:T(8,128)S(1)}, f32[1,1,64,128]{3,2,1,0:T(8,128)S(1)}, u32[]{:S(2)}, u32[]{:S(2)}) collective-permute-start(f32[1,1,64,128]{3,2,1,0:T(8,128)S(1)} %get-tuple-element.19), channel_id=1, source_target_pairs={{0,1},{1,2},{2,3},{4,5},{5,6},{6,7},{8,9},{9,10},{10,11},{12,13},{... | collective-permute-start | bytes 98312 | tf_op jit(solution)/shard_map/ppermute | solution.py:24
  107.7 9.6 %collective-permute-start.15 = (f32[1,1,64,128]{3,2,1,0:T(8,128)S(1)}, f32[1,1,64,128]{3,2,1,0:T(8,128)S(1)}, u32[]{:S(2)}, u32[]{:S(2)}) collective-permute-start(f32[1,1,64,128]{3,2,1,0:T(8,128)S(1)} %get-tuple-element.18), channel_id=1, source_target_pairs={{1,0},{2,1},{3,2},{5,4},{6,5},{7,6},{9,8},{10,9},{11,10},{13,12},{... | collective-permute-start | bytes 98312 | tf_op jit(solution)/shard_map/ppermute | solution.py:26
  109.7 8.6 %collective-permute-start.16 = (f32[1,1,64,128]{3,2,1,0:T(8,128)S(1)}, f32[1,1,64,128]{3,2,1,0:T(8,128)S(1)}, u32[]{:S(2)}, u32[]{:S(2)}) collective-permute-start(f32[1,1,64,128]{3,2,1,0:T(8,128)S(1)} %get-tuple-element.17), channel_id=1, source_target_pairs={{0,1},{1,2},{2,3},{4,5},{5,6},{6,7},{8,9},{9,10},{10,11},{12,13},{... | collective-permute-start | bytes 98312 | tf_op jit(solution)/shard_map/ppermute | solution.py:24
  119.8 10.4 %collective-permute-start.17 = (f32[2,1,32,128]{3,2,1,0:T(8,128)S(1)}, f32[2,1,32,128]{3,2,1,0:T(8,128)S(1)}, u32[]{:S(2)}, u32[]{:S(2)}) collective-permute-start(f32[2,1,32,128]{3,2,1,0:T(8,128)S(1)} %get-tuple-element.34), channel_id=1, source_target_pairs={{1,0},{2,1},{3,2},{5,4},{6,5},{7,6},{9,8},{10,9},{11,10},{13,12},{... | collective-permute-start | bytes 98312 | tf_op jit(solution)/shard_map/ppermute | solution.py:26
  121.8 9.1 %collective-permute-start.18 = (f32[2,1,32,128]{3,2,1,0:T(8,128)S(1)}, f32[2,1,32,128]{3,2,1,0:T(8,128)S(1)}, u32[]{:S(2)}, u32[]{:S(2)}) collective-permute-start(f32[2,1,32,128]{3,2,1,0:T(8,128)S(1)} %get-tuple-element.33), channel_id=1, source_target_pairs={{0,1},{1,2},{2,3},{4,5},{5,6},{6,7},{8,9},{9,10},{10,11},{12,13},{... | collective-permute-start | bytes 98312 | tf_op jit(solution)/shard_map/ppermute | solution.py:24
  (14 other events, 69.6 us)
where the time goes:
time: 133 us; the launch traced here: 132 us
  starting transfers between devices  93.2 us (70%)
  waiting for transfers between devices  16.3 us (12%)
  other arithmetic  15.3 us (12%)
  local copies, waits for them, and re-layouts  6.78 us (5%)
    ppermute x9, starting transfers between devices, extended(): lax.ppermute(tail, axis, [(i, (i + 1) % count) for i in range(ends)])  72 us
    ppermute x9, starting transfers between devices, extended(): lax.ppermute(head, axis, [((i + 1) % count, i) for i in range(ends)])  17.9 us
    ppermute x1, waiting for transfers between devices, passed_along(): return lax.ppermute(array, axis, pairs)  11.3 us
    ppermute x9, waiting for transfers between devices, extended(): lax.ppermute(tail, axis, [(i, (i + 1) % count) for i in range(ends)])  4.91 us
    unnamed x43, local copies, waits for them, and re-layouts  3.44 us
    ppermute x1, starting transfers between devices, passed_along(): return lax.ppermute(array, axis, pairs)  3.19 us
    reduce_sum x9, other arithmetic, restrict(): return 0.25 * jnp.sum(blocks, axis=(-4, -2))  2.67 us
  transfers between devices with their start and end apart: 19, of which 7 were waited for; matrix products, arithmetic and copies ran while one was open for 5% of the time, Pallas kernels for 0%

commit v1 on v0

v1 whole, which is shorter than its diff:
```python
import functools

import jax
import jax.numpy as jnp
from jax import lax
from jax.experimental import pallas as pl
from jax.experimental.pallas import tpu as pltpu
from jax.sharding import PartitionSpec as P

F32 = jnp.float32
H = 0.5
SLAB = 8
NY = 64
NZ = 128
PLANE = (NY, NZ)
ROWS = NY // 2

VM = pl.BlockSpec(memory_space=pltpu.VMEM)
SM = pl.BlockSpec(memory_space=pltpu.SMEM)
ANY = pl.BlockSpec(memory_space=pl.ANY)


def planes(count, rows=NY):
    return jax.ShapeDtypeStruct((count, rows, NZ), F32)


def grid_masks():
    row = lax.broadcasted_iota(jnp.int32, PLANE, 0)
    lane = lax.broadcasted_iota(jnp.int32, PLANE, 1)
    return row, lane


def shift_rows(v, by, row):
    rolled = pltpu.roll(v, (-by) % NY, 0)
    if by > 0:
        return jnp.where(row < NY - by, rolled, 0.0)
    return jnp.where(row >= -by, rolled, 0.0)


def shift_lanes(v, by, lane):
    rolled = pltpu.roll(v, (-by) % NZ, 1)
    if by > 0:
        return jnp.where(lane < NZ - by, rolled, 0.0)
    return jnp.where(lane >= -by, rolled, 0.0)


def fine_laplace(before, here, after, masks):
    row, lane = masks
    total = before + after
    total = total + (shift_rows(here, 1, row) + shift_rows(here, -1, row))
    total = total + (shift_lanes(here, 1, lane) + shift_lanes(here, -1, lane))
    return total - 6.0 * here


def driving(before, here, after, slow, conduct, threshold, masks):
    local = 2.0 * here * (1.0 - here) * (here - threshold) - slow
    return conduct * fine_laplace(before, here, after, masks) + local


def relaxing(here, slow, recovery):
    return recovery * (here - 0.5 * slow)


def pair_mean(v, row):
    other = jnp.where(row % 2 == 0, pltpu.roll(v, NY - 1, 0), pltpu.roll(v, 1, 0))
    return 0.25 * (v + other)


def coarse_laplace_inside(here, masks):
    row, lane = masks
    along_y = shift_rows(here, 2, row) + shift_rows(here, -2, row) - 2.0 * here
    along_z = shift_lanes(here, 1, lane) + shift_lanes(here, -1, lane) - 2.0 * here
    return 0.25 * along_y + along_z - 0.5 * here


def loop(count, body):
    def step(i, carry):
        body(i)
        return carry

    lax.fori_loop(0, count, step, 0)


def pack_kernel(core_ref, start, conduct, threshold, recovery, to_a, to_b, sem):
    core = core_ref[0]
    moves = []
    for pay, right in ((to_a, core == 0), (to_b, core == 1)):
        at = 0
        for src, width in (
            (start.at[0, 0], 5),
            (start.at[0, 1], 4),
            (conduct, 4),
            (threshold, 4),
            (recovery, 3),
        ):
            off = jnp.where(right, SLAB - width, 0)
            moves.append(
                pltpu.make_async_copy(
                    src.at[pl.ds(off, width)], pay.at[pl.ds(at, width)], sem.at[len(moves)]
                )
            )
            at += width
    for move in moves:
        move.start()
    for move in moves:
        move.wait()


def copy_planes(dst, at, src, first, count):
    dst[pl.ds(at, count)] = src[pl.ds(first, count)]


def sides(core, ra, rb, fill):
    @pl.when(core == 0)
    def _():
        fill(rb, ra)

    @pl.when(core == 1)
    def _():
        fill(ra, rb)


def first_kernel(
    core_ref, start, conduct, threshold, recovery, ra, rb,
    u2, dpay, bpay, apay, e, r, c, th, rc, f0e, f0r, n1e, n1r, n2e, n2r, d1e, d1r, dle, dlr,
    f1e, f1r, rse, rsr, line,
):
    core = core_ref[0]
    masks = grid_masks()
    row = masks[0]
    for dst, at, src in ((e, 5, start.at[0, 0]), (r, 4, start.at[0, 1]), (c, 4, conduct), (th, 4, threshold), (rc, 4, recovery)):
        copy_planes(dst, at, src, 0, SLAB)

    def fill(left, right):
        for halo, hi in ((left, False), (right, True)):
            copy_planes(e, 13 if hi else 0, halo, 0, 5)
            copy_planes(r, 12 if hi else 0, halo, 5, 4)
            copy_planes(c, 12 if hi else 0, halo, 9, 4)
            copy_planes(th, 12 if hi else 0, halo, 13, 4)
            copy_planes(rc, 12 if hi else 1, halo, 17, 3)

    sides(core, ra, rb, fill)
    rc[0] = jnp.zeros(PLANE, F32)
    rc[15] = jnp.zeros(PLANE, F32)

    def one(i):
        here, slow = e[i + 1], r[i]
        fe = driving(e[i], here, e[i + 2], slow, c[i], th[i], masks)
        fr = relaxing(here, slow, rc[i])
        f0e[i] = fe
        f0r[i] = fr
        n1e[i] = here + H * fe
        n1r[i] = slow + H * fr

    loop(16, one)

    def two(i):
        here, slow = n1e[i + 1], n1r[i + 1]
        fe = driving(n1e[i], here, n1e[i + 2], slow, c[i + 1], th[i + 1], masks)
        fr = relaxing(here, slow, rc[i + 1])
        f1e[i] = fe
        f1r[i] = fr
        n2e[i] = here + H * fe
        n2r[i] = slow + H * fr

    loop(14, two)

    def three(k):
        jump_e = jump_r = sum_e = sum_r = 0.0
        for half in range(2):
            i = 2 * k + half
            here, slow = n2e[i + 1], n2r[i + 1]
            fe = driving(n2e[i], here, n2e[i + 2], slow, c[i + 2], th[i + 2], masks)
            fr = relaxing(here, slow, rc[i + 2])
            jump_e += (-7.0 / 24.0) * f0e[i + 2] + (1.0 / 3.0) * f1e[i + 1] - (1.0 / 24.0) * fe
            jump_r += (-7.0 / 24.0) * f0r[i + 2] + (1.0 / 3.0) * f1r[i + 1] - (1.0 / 24.0) * fr
            sum_e += (-1.0 / 24.0) * f0e[i + 2] + (1.0 / 3.0) * f1e[i + 1] + (5.0 / 24.0) * fe
            sum_r += (-1.0 / 24.0) * f0r[i + 2] + (1.0 / 3.0) * f1r[i + 1] + (5.0 / 24.0) * fr
        d1e[k] = pair_mean(jump_e, row)
        d1r[k] = pair_mean(jump_r, row)
        rse[k] = pair_mean(sum_e, row)
        rsr[k] = pair_mean(sum_r, row)

    loop(6, three)

    def four(k):
        i = 2 * k
        mean = lambda ref, at: pair_mean(ref[at + i] + ref[at + i + 1], row)
        gc, gt, gr = mean(c, 4), mean(th, 4), mean(rc, 4)
        be, br = mean(n1e, 4), mean(n1r, 4)
        de, dr = d1e[k + 1], d1r[k + 1]
        ce, cr = be + de, br + dr
        lap = coarse_laplace_inside(de, masks) + 0.25 * (d1e[k] + d1e[k + 2])
        ge = gc * lap + 2.0 * (ce * (1.0 - ce) * (ce - gt) - be * (1.0 - be) * (be - gt)) - dr
        g_r = gr * (de - 0.5 * dr)
        xe = ce + H * ge + rse[k + 1] - mean(n2e, 3)
        xr = cr + H * g_r + rsr[k + 1] - mean(n2r, 3)
        dle[k] = xe
        dlr[k] = xr
        for half in range(2):
            u2[0, i + half] = n2e[i + 3 + half] + xe
            u2[1, i + half] = n2r[i + 3 + half] + xr

    loop(4, four)

    def edges(right, pay, with_d):
        lo = 5 if right else 0
        if with_d:
            copy_planes(dpay, 0, u2.at[0], 5 if right else 0, 3)
            copy_planes(dpay, 3, u2.at[1], 6 if right else 0, 2)
        picks = (
            ((d1e, 3), (dle, 2), (dle, 3), (dlr, 3)) if right else ((d1e, 2), (dle, 0), (dle, 1), (dlr, 0))
        )
        for at, (ref, k) in enumerate(picks):
            pay[at] = ref[k, pl.ds(0, ROWS, stride=2), :]

    @pl.when(core == 0)
    def _():
        edges(True, apay, False)
        edges(False, bpay, True)

    @pl.when(core == 1)
    def _():
        edges(False, apay, False)
        edges(True, bpay, True)


def doubled(dst, k, src, at):
    v = src[at]
    dst[k, pl.ds(0, ROWS, stride=2), :] = v
    dst[k, pl.ds(1, ROWS, stride=2), :] = v


def middle_kernel(
    core_ref, ra, rb, c, th, rc, f0e, f0r, n1e, n1r, n2e, n2r, d1e, d1r, dle, dlr,
    k1e, k1r, k2e, k2r,
    u1e, u1r, u2e, u2r, xd1e, xdle, xdlr,
):
    core = core_ref[0]
    masks = grid_masks()
    copy_planes(xd1e, 1, d1e, 0, 6)
    copy_planes(xdle, 2, dle, 0, 4)
    copy_planes(xdlr, 1, dlr, 0, 4)

    def fill(left, right):
        doubled(xd1e, 0, left, 0)
        doubled(xdle, 0, left, 1)
        doubled(xdle, 1, left, 2)
        doubled(xdlr, 0, left, 3)
        doubled(xd1e, 7, right, 0)
        doubled(xdle, 6, right, 1)
        doubled(xdle, 7, right, 2)
        doubled(xdlr, 5, right, 3)

    sides(core, ra, rb, fill)

    def states_e(i):
        k = (i + 1) // 2
        u1e[i] = n1e[i + 1] + xd1e[k]
        u2e[i] = n2e[i] + xdle[k]

    loop(14, states_e)

    def states_r(i):
        k = i // 2
        u1r[i] = n1r[i + 2] + d1r[k]
        u2r[i] = n2r[i + 1] + xdlr[k]

    loop(12, states_r)

    def terms(i):
        fe = (
            driving(u1e[i], u1e[i + 1], u1e[i + 2], u1r[i], c[i + 2], th[i + 2], masks),
            driving(u2e[i], u2e[i + 1], u2e[i + 2], u2r[i], c[i + 2], th[i + 2], masks),
        )
        fr = (relaxing(u1e[i + 1], u1r[i], rc[i + 2]), relaxing(u2e[i + 1], u2r[i], rc[i + 2]))
        for f0, f, k1, k2 in ((f0e, fe, k1e, k2e), (f0r, fr, k1r, k2r)):
            base = f0[i + 2]
            k1[i] = (-7.0 / 24.0) * base + (1.0 / 3.0) * f[0] - (1.0 / 24.0) * f[1]
            k2[i] = (-1.0 / 24.0) * base - (1.0 / 6.0) * f[0] + (5.0 / 24.0) * f[1]

    loop(12, terms)


def edge_kernel(core_ref, q, pay):
    @pl.when(core_ref[0] == 0)
    def _():
        copy_planes(pay, 0, q.at[0], 5, 3)
        copy_planes(pay, 3, q.at[1], 6, 2)

    @pl.when(core_ref[0] == 1)
    def _():
        copy_planes(pay, 0, q.at[0], 0, 3)
        copy_planes(pay, 3, q.at[1], 0, 2)


def second_kernel(
    core_ref, head_ref, q, qa, qb, e, r, c, th, rc, k1e, k1r, k2e, k2r,
    apay, bpay, base, d1e, coef,
    qe, qr, fqe, fqr, n1e, n1r, f1e, f1r, n2e, n2r, d1r, rse, rsr,
):
    core = core_ref[0]
    masks = grid_masks()
    row = masks[0]

    @pl.when(head_ref[0] == 1)
    def _():
        copy_planes(qe, 0, e, 2, 14)
        copy_planes(qr, 0, r, 2, 12)

    @pl.when(head_ref[0] == 0)
    def _():
        copy_planes(qe, 3, q.at[0], 0, SLAB)
        copy_planes(qr, 2, q.at[1], 0, SLAB)

        def fill(left, right):
            copy_planes(qe, 0, left, 0, 3)
            copy_planes(qr, 0, left, 3, 2)
            copy_planes(qe, 11, right, 0, 3)
            copy_planes(qr, 10, right, 3, 2)

        sides(core, qa, qb, fill)

    def one(i):
        here, slow = qe[i + 1], qr[i]
        fe = driving(qe[i], here, qe[i + 2], slow, c[i + 2], th[i + 2], masks)
        fr = relaxing(here, slow, rc[i + 2])
        fqe[i] = fe
        fqr[i] = fr
        n1e[i] = here + H * fe + k1e[i]
        n1r[i] = slow + H * fr + k1r[i]

    loop(12, one)

    def two(i):
        here, slow = n1e[i + 1], n1r[i + 1]
        fe = driving(n1e[i], here, n1e[i + 2], slow, c[i + 3], th[i + 3], masks)
        fr = relaxing(here, slow, rc[i + 3])
        f1e[i] = fe
        f1r[i] = fr
        n2e[i] = here + H * fe + k2e[i + 1]
        n2r[i] = slow + H * fr + k2r[i + 1]

    loop(10, two)

    def three(k):
        jump_e = jump_r = sum_e = sum_r = 0.0
        for half in range(2):
            i = 2 * k + half
            here, slow = n2e[i + 1], n2r[i + 1]
            fe = driving(n2e[i], here, n2e[i + 2], slow, c[i + 4], th[i + 4], masks)
            fr = relaxing(here, slow, rc[i + 4])
            fq, f1 = fqe[i + 2], f1e[i + 1]
            jump_e += (qe[i + 3] - n1e[i + 2]) + (5.0 / 24.0) * fq + (1.0 / 3.0) * f1 - (1.0 / 24.0) * fe
            sum_e += (-1.0 / 24.0) * fq + (1.0 / 3.0) * f1 + (5.0 / 24.0) * fe
            fq, f1 = fqr[i + 2], f1r[i + 1]
            jump_r += (qr[i + 2] - n1r[i + 2]) + (5.0 / 24.0) * fq + (1.0 / 3.0) * f1 - (1.0 / 24.0) * fr
            sum_r += (-1.0 / 24.0) * fq + (1.0 / 3.0) * f1 + (5.0 / 24.0) * fr
        d1e[k + 1] = pair_mean(jump_e, row)
        d1r[k] = pair_mean(jump_r, row)
        rse[k] = pair_mean(sum_e, row)
        rsr[k] = pair_mean(sum_r, row)

    loop(4, three)
    d1e[0] = jnp.zeros(PLANE, F32)
    d1e[5] = jnp.zeros(PLANE, F32)

    @pl.when(core == 0)
    def _():
        apay[0] = d1e[4, pl.ds(0, ROWS, stride=2), :]
        bpay[0] = d1e[1, pl.ds(0, ROWS, stride=2), :]

    @pl.when(core == 1)
    def _():
        apay[0] = d1e[1, pl.ds(0, ROWS, stride=2), :]
        bpay[0] = d1e[4, pl.ds(0, ROWS, stride=2), :]

    def four(k):
        i = 2 * k
        mean = lambda ref, at: pair_mean(ref[at + i] + ref[at + i + 1], row)
        gc, gt, gr = mean(c, 4), mean(th, 4), mean(rc, 4)
        be, br = mean(n1e, 2), mean(n1r, 2)
        de, dr = d1e[k + 1], d1r[k]
        ce, cr = be + de, br + dr
        lap = coarse_laplace_inside(de, masks) + 0.25 * (d1e[k] + d1e[k + 2])
        ge = gc * lap + 2.0 * (ce * (1.0 - ce) * (ce - gt) - be * (1.0 - be) * (be - gt)) - dr
        g_r = gr * (de - 0.5 * dr)
        xe = ce + H * ge + rse[k] - mean(n2e, 1)
        xr = cr + H * g_r + rsr[k] - mean(n2r, 1)
        coef[k] = (0.25 * H) * gc
        for half in range(2):
            base[0, i + half] = n2e[i + 1 + half] + xe
            base[1, i + half] = n2r[i + 1 + half] + xr

    loop(4, four)


def last_kernel(core_ref, base, coef, ra, rb, out, wide):
    def fill(left, right):
        doubled(wide, 0, left, 0)
        doubled(wide, 1, right, 0)

    sides(core_ref[0], ra, rb, fill)
    out[0] = base[...]
    for side, k in ((0, 0), (1, 3)):
        add = coef[k] * wide[side]
        for half in range(2):
            out[0, 0, 2 * k + half] = base[0, 2 * k + half] + add


def call(kernel, out_shape, scratch=(), in_specs=None, out_specs=None, **kw):
    return pl.pallas_call(
        kernel,
        out_shape=out_shape,
        in_specs=in_specs,
        out_specs=out_specs,
        scratch_shapes=[pltpu.VMEM(s, F32) if isinstance(s, tuple) else s for s in scratch],
        compiler_params=pltpu.CompilerParams(vmem_limit_bytes=24 << 20),
        **kw,
    )


def per_device(start, conduct, threshold, recovery):
    steps = lax.axis_size("tm")
    space = lax.axis_size("space")
    place = lax.axis_index("space")
    core = (place % 2).reshape(1).astype(jnp.int32)
    head = (lax.axis_index("tm") == 0).reshape(1).astype(jnp.int32)

    chip_pairs = [(s, s ^ 1) for s in range(space)]
    link_pairs = [(s, s + 1) for s in range(1, space - 1, 2)] + [(s + 1, s) for s in range(1, space - 1, 2)]
    next_pairs = [(p, p + 1) for p in range(steps - 1)]
    slant_pairs = [(p * space + a, (p + 1) * space + b) for p in range(steps - 1) for a, b in link_pairs]
    on_chip = lambda v: lax.ppermute(v, "space", chip_pairs)
    on_link = lambda v: lax.ppermute(v, "space", link_pairs)

    to_a, to_b = call(
        pack_kernel,
        (planes(20), planes(20)),
        [pltpu.SemaphoreType.DMA((10,))],
        in_specs=[SM, ANY, ANY, ANY, ANY],
        out_specs=(VM, VM),
    )(core, start, conduct, threshold, recovery)
    got_b = on_link(to_b)
    got_a = on_chip(to_a)

    (u2, dpay, bpay, apay, e, r, c, th, rc, f0e, f0r, n1e, n1r, n2e, n2r, d1e, d1r, dle, dlr) = call(
        first_kernel,
        (jax.ShapeDtypeStruct((2, SLAB) + PLANE, F32), planes(5), planes(4, ROWS), planes(4, ROWS))
        + (planes(18), planes(16), planes(16), planes(16), planes(16))
        + (planes(16),) * 4
        + (planes(14),) * 2
        + (planes(6),) * 2
        + (planes(4),) * 2,
        [(14,) + PLANE] * 2 + [(6,) + PLANE] * 2 + [PLANE],
        in_specs=[SM] + [VM] * 6,
        out_specs=(VM,) * 19,
    )(core, start, conduct, threshold, recovery, got_a, got_b)

    q = lax.ppermute(u2, "tm", next_pairs)
    q_b = lax.ppermute(dpay, ("tm", "space"), slant_pairs)
    fix_b = on_link(bpay)
    fix_a = on_chip(apay)

    k_terms = call(
        middle_kernel,
        (planes(12),) * 4,
        [(14,) + PLANE, (12,) + PLANE] * 2 + [(8,) + PLANE] * 2 + [(6,) + PLANE],
        in_specs=[SM] + [VM] * 15,
        out_specs=(VM,) * 4,
    )(core, fix_a, fix_b, c, th, rc, f0e, f0r, n1e, n1r, n2e, n2r, d1e, d1r, dle, dlr)

    q_pay = call(edge_kernel, planes(5), in_specs=[SM, VM], out_specs=VM)(core, q)
    q_a = on_chip(q_pay)

    apay, bpay, base, d1, coef = call(
        second_kernel,
        (planes(1, ROWS), planes(1, ROWS), jax.ShapeDtypeStruct((2, SLAB) + PLANE, F32), planes(6), planes(4)),
        [(14,) + PLANE] + [(12,) + PLANE] * 5 + [(10,) + PLANE] * 4 + [(4,) + PLANE] * 3,
        in_specs=[SM, SM] + [VM] * 12,
        out_specs=(VM,) * 5,
    )(core, head, q, q_a, q_b, e, r, c, th, rc, *k_terms)

    jump_b = on_link(bpay)
    jump_a = on_chip(apay)
    return call(
        last_kernel,
        jax.ShapeDtypeStruct((1, 2, SLAB) + PLANE, F32),
        [(2,) + PLANE],
        in_specs=[SM] + [VM] * 4,
        out_specs=VM,
    )(core, base, coef, jump_a, jump_b)


def solution(mesh):
    placed = (
        P("tm", None, "space", None, None),
        P("space", None, None),
        P("space", None, None),
        P("space", None, None),
    )
    return jax.shard_map(
        per_device,
        mesh=mesh,
        in_specs=placed,
        out_specs=P("tm", None, "space", None, None),
        check_vma=False,
    )
```

time: 133 us -> 95.7 us (0.72)
  starting transfers between devices: 93.2 us -> 37.7 us
  Pallas kernels: 0 us -> 16.2 us
  other arithmetic: 15.3 us -> 0 us
  local copies, waits for them, and re-layouts: 6.78 us -> 16.7 us
  waiting for transfers between devices: 16.3 us -> 24.2 us
    ppermute x19 -> x9, starting transfers between devices: 93.2 us -> 37.7 us  [the longest x3 24.3 us: per_device(): on_link = lambda v: lax.ppermute(v, 'space', link_pairs)]
    pallas_call x0 -> x6, Pallas kernels: none -> 16.2 us  [the longest x1 5.24 us: per_device(): call(first_kernel, (jax.ShapeDtypeStruct((2, SLAB) + PLANE, F32), planes(...]
    unnamed x43 -> x40, local copies, waits for them, and re-layouts: 3.44 us -> 16.7 us
    ppermute x19 -> x9, waiting for transfers between devices: 16.3 us -> 24.2 us  [the longest x3 13 us: per_device(): on_link = lambda v: lax.ppermute(v, 'space', link_pairs)]
    reduce_sum x9 -> x0, other arithmetic: 2.67 us -> none  [restrict(): return 0.25 * jnp.sum(blocks, axis=(-4, -2))]
    add x8 -> x0, other arithmetic: 2.51 us -> none  [the longest x2 1.35 us: per_device(): node_two_new = node_two + prolong(coarse_jump)]
    concatenate x9 -> x0, other arithmetic: 2.39 us -> none  [extended(): jnp.concatenate([lax.ppermute(tail, axis, [(i, (i + 1) % count) for i in...]
    sub x8 -> x0, other arithmetic: 2.26 us -> none  [the longest x6 2.1 us: forces(): conduct * laplace]
  transfers between devices with their start and end apart: 19 -> 9, of which waited for: 7 -> 4; matrix products, arithmetic and copies ran while one was open for 5% -> 0% of each run, Pallas kernels for 0% -> 3%
where the time goes in v1:
time: 95.7 us; the launch traced here: 94.9 us
  starting transfers between devices  37.7 us (39%)
  waiting for transfers between devices  24.2 us (25%)
  local copies, waits for them, and re-layouts  16.7 us (17%)
  Pallas kernels  16.2 us (17%)
    ppermute x3, starting transfers between devices, per_device(): on_link = lambda v: lax.ppermute(v, 'space', link_pairs)  24.3 us
    unnamed x40, local copies, waits for them, and re-layouts  16.7 us
    ppermute x3, waiting for transfers between devices, per_device(): on_link = lambda v: lax.ppermute(v, 'space', link_pairs)  13 us
    ppermute x1, waiting for transfers between devices, per_device(): q = lax.ppermute(u2, 'tm', next_pairs)  11.2 us
    ppermute x1, starting transfers between devices, per_device(): q_b = lax.ppermute(dpay, ('tm', 'space'), slant_pairs)  8.97 us
    pallas_call x1, Pallas kernels, per_device(): call(first_kernel, (jax.ShapeDtypeStruct((2, SLAB) + PLANE, F32), planes(...  5.24 us
    pallas_call x1, Pallas kernels, per_device(): call(second_kernel, (planes(1, ROWS), planes(1, ROWS), jax.ShapeDtypeStru...  5.03 us
    ppermute x1, starting transfers between devices, per_device(): q = lax.ppermute(u2, 'tm', next_pairs)  3.19 us
  transfers between devices with their start and end apart: 9, of which 4 were waited for; matrix products, arithmetic and copies ran while one was open for 0% of the time, Pallas kernels for 3%

profile of v1, /device:TPU:7, one launch (start us, length us, event | category | flops | bytes accessed | tf_op | source)
XLA Modules:
  0.0 94.9 jit_solution(17981750210371007756)
XLA Ops:
  0.0 1.0 %copy-done = f32[1,2,8,64,128]{4,3,2,1,0:T(8,128)S(1)} copy-done((f32[1,2,8,64,128]{4,3,2,1,0:T(8,128)S(1)}, f32[1,2,8,64,128]{4,3,2,1,0:T(8,128)}, u32[]{:S(2)}) %copy-start) | copy-done | bytes 524312
  1.0 0.9 copy-done.1
  2.0 0.9 copy-done.2
  2.9 0.9 copy-done.3
  3.9 1.8 %shard_map.46 = (f32[20,64,128]{2,1,0:T(8,128)S(1)}, f32[20,64,128]{2,1,0:T(8,128)S(1)}) custom-call(s32[1]{0:T(128)} %bitcast.core_ref, f32[1,2,8,64,128]{4,3,2,1,0:T(8,128)S(1)} %copy-done, f32[8,64,128]{2,1,0:T(8,128)S(1)} %copy-done.1, f32[8,64,128]{2,1,0:T(8,128)S(1)} %copy-done.2, f32[8,64,128]{2,1,0:T(8,128)S(1)} %copy-done.3), custom_call_target="tpu_custom_call" | custom-call | tf_op jit(solution)/shard_map/pallas_call | solution.py:437
  6.4 8.7 %collective-permute-start.1 = (f32[20,64,128]{2,1,0:T(8,128)S(1)}, f32[20,64,128]{2,1,0:T(8,128)S(1)}, u32[]{:S(2)}, u32[]{:S(2)}) collective-permute-start(f32[20,64,128]{2,1,0:T(8,128)S(1)} %get-tuple-element.35), channel_id=1, source_target_pairs={{1,2},{2,1},{5,6},{6,5},{9,10},{10,9},{13,14},{14,13},{17,18},{18,... | collective-permute-start | bytes 1966088 | tf_op jit(solution)/shard_map/ppermute | solution.py:435
  15.2 9.4 %collective-permute-done.1.rb = f32[20,64,128]{2,1,0:T(8,128)S(1)} collective-permute-done((f32[20,64,128]{2,1,0:T(8,128)S(1)}, f32[20,64,128]{2,1,0:T(8,128)S(1)}, u32[]{:S(2)}, u32[]{:S(2)}) %collective-permute-start.1) | collective-permute-done | bytes 655392 | tf_op jit(solution)/shard_map/ppermute | solution.py:435
  24.6 5.2 %shard_map.47 = (f32[2,8,64,128]{3,2,1,0:T(8,128)S(1)}, f32[5,64,128]{2,1,0:T(8,128)}, f32[4,32,128]{2,1,0:T(8,128)}, f32[4,32,128]{2,1,0:T(8,128)}, f32[18,64,1...) custom-call(s32[1]{0:T(128)} %bitcast.core_ref, ...), custom_call_target="tpu_custom_call" | custom-call | tf_op jit(solution)/shard_map/pallas_call | solution.py:447
  34.6 3.2 %collective-permute-start.2 = (f32[2,8,64,128]{3,2,1,0:T(8,128)S(1)}, f32[2,8,64,128]{3,2,1,0:T(8,128)S(1)}, u32[]{:S(2)}, u32[]{:S(2)}) collective-permute-start(f32[2,8,64,128]{3,2,1,0:T(8,128)S(1)} %get-tuple-element.36), channel_id=1, source_target_pairs={{0,4},{4,8},{8,12},{12,16},{16,20},{20,24},{24,28},{28,32},{32,36}... | collective-permute-start | bytes 1572872 | tf_op jit(solution)/shard_map/ppermute | solution.py:460
  37.8 9.0 %collective-permute-start.4 = (f32[5,64,128]{2,1,0:T(8,128)}, f32[5,64,128]{2,1,0:T(8,128)}, u32[]{:S(2)}, u32[]{:S(2)}) collective-permute-start(f32[5,64,128]{2,1,0:T(8,128)} %get-tuple-element.37), channel_id=1, source_target_pairs={{1,6},{2,5},{5,10},{6,9},{9,14},{10,13},{13,18},{14,17},{17,22},{1... | collective-permute-start | bytes 491528 | tf_op jit(solution)/shard_map/ppermute | solution.py:461
  46.8 11.2 %collective-permute-done.2.q = f32[2,8,64,128]{3,2,1,0:T(8,128)S(1)} collective-permute-done((f32[2,8,64,128]{3,2,1,0:T(8,128)S(1)}, f32[2,8,64,128]{3,2,1,0:T(8,128)S(1)}, u32[]{:S(2)}, u32[]{:S(2)}) %collective-permute-start.2) | collective-permute-done | bytes 524320 | tf_op jit(solution)/shard_map/ppermute | solution.py:460
  59.1 8.0 %collective-permute-start.6 = (f32[4,32,128]{2,1,0:T(8,128)}, f32[4,32,128]{2,1,0:T(8,128)}, u32[]{:S(2)}, u32[]{:S(2)}) collective-permute-start(f32[4,32,128]{2,1,0:T(8,128)} %get-tuple-element.44), channel_id=1, source_target_pairs={{1,2},{2,1},{5,6},{6,5},{9,10},{10,9},{13,14},{14,13},{17,18},{18,... | collective-permute-start | bytes 196616 | tf_op jit(solution)/shard_map/ppermute | solution.py:435
  67.2 2.2 %collective-permute-done.6.rb = f32[4,32,128]{2,1,0:T(8,128)} collective-permute-done((f32[4,32,128]{2,1,0:T(8,128)}, f32[4,32,128]{2,1,0:T(8,128)}, u32[]{:S(2)}, u32[]{:S(2)}) %collective-permute-start.6) | collective-permute-done | bytes 65568 | tf_op jit(solution)/shard_map/ppermute | solution.py:435
  69.4 1.0 %copy-done.5 = f32[16,64,128]{2,1,0:T(8,128)S(1)} copy-done((f32[16,64,128]{2,1,0:T(8,128)S(1)}, f32[16,64,128]{2,1,0:T(8,128)}, u32[]{:S(2)}) %copy-start.5) | copy-done | bytes 524312
  70.4 1.0 %copy-done.7 = f32[16,64,128]{2,1,0:T(8,128)S(1)} copy-done((f32[16,64,128]{2,1,0:T(8,128)S(1)}, f32[16,64,128]{2,1,0:T(8,128)}, u32[]{:S(2)}) %copy-start.7) | copy-done | bytes 524312
  71.5 1.0 %copy-done.9 = f32[16,64,128]{2,1,0:T(8,128)S(1)} copy-done((f32[16,64,128]{2,1,0:T(8,128)S(1)}, f32[16,64,128]{2,1,0:T(8,128)}, u32[]{:S(2)}) %copy-start.9) | copy-done | bytes 524312
  72.5 1.0 %copy-done.11 = f32[16,64,128]{2,1,0:T(8,128)S(1)} copy-done((f32[16,64,128]{2,1,0:T(8,128)S(1)}, f32[16,64,128]{2,1,0:T(8,128)}, u32[]{:S(2)}) %copy-start.11) | copy-done | bytes 524312
  73.6 1.0 %copy-done.13 = f32[14,64,128]{2,1,0:T(8,128)S(1)} copy-done((f32[14,64,128]{2,1,0:T(8,128)S(1)}, f32[14,64,128]{2,1,0:T(8,128)}, u32[]{:S(2)}) %copy-start.13) | copy-done | bytes 458776
  74.6 1.0 %copy-done.15 = f32[14,64,128]{2,1,0:T(8,128)S(1)} copy-done((f32[14,64,128]{2,1,0:T(8,128)S(1)}, f32[14,64,128]{2,1,0:T(8,128)}, u32[]{:S(2)}) %copy-start.15) | copy-done | bytes 458776
  75.6 0.9 copy-done.17
  77.4 2.6 %shard_map.49 = (f32[12,64,128]{2,1,0:T(8,128)S(1)}, f32[12,64,128]{2,1,0:T(8,128)S(1)}, f32[12,64,128]{2,1,0:T(8,128)S(1)}, f32[12,64,128]{2,1,0:T(8,128)S(1)}) custom-call(s32[1]{0:T(128)} %bitcast.core_ref, f32[4,32,128]{2,1,0:T(8,128)} %collective-permute-done.5.ra, f32[4,32,128]{2,1,0:T(8,128)} %collective-permute-done.6.rb, ...), custom_call_target="tpu_custom_call" | custom-call | tf_op jit(solution)/shard_map/pallas_call | solution.py:465
  80.1 5.0 %shard_map.50 = (f32[1,32,128]{2,1,0:T(8,128)S(1)}, f32[1,32,128]{2,1,0:T(8,128)S(1)}, f32[2,8,64,128]{3,2,1,0:T(8,128)S(1)}, f32[6,64,128]{2,1,0:T(8,128)}, f32[4,64,128]{2,1,0:T(8,128)S(1)}) custom-call(s32[1]{0:T(128)} %bitcast.core_ref, s32[1]{0:T(128)} %bitcast.1.head_ref, f32[2,8,64,128]{3,2,1,0:T(8,128)S(1)} %collective-permute-done.2.q, ...), custom_call_target="tpu_custom_call" | custom-call | tf_op jit(solution)/shard_map/pallas_call | solution.py:476
  85.1 7.5 %collective-permute-start.8 = (f32[1,32,128]{2,1,0:T(8,128)S(1)}, f32[1,32,128]{2,1,0:T(8,128)S(1)}, u32[]{:S(2)}, u32[]{:S(2)}) collective-permute-start(f32[1,32,128]{2,1,0:T(8,128)S(1)} %get-tuple-element.62), channel_id=1, source_target_pairs={{1,2},{2,1},{5,6},{6,5},{9,10},{10,9},{13,14},{14,13},{17,18},{18,... | collective-permute-start | bytes 49160 | tf_op jit(solution)/shard_map/ppermute | solution.py:435
  92.7 1.4 %collective-permute-done.8.rb = f32[1,32,128]{2,1,0:T(8,128)S(1)} collective-permute-done((f32[1,32,128]{2,1,0:T(8,128)S(1)}, f32[1,32,128]{2,1,0:T(8,128)S(1)}, u32[]{:S(2)}, u32[]{:S(2)}) %collective-permute-start.8) | collective-permute-done | bytes 16416 | tf_op jit(solution)/shard_map/ppermute | solution.py:435
  (40 shorter events, 8.5 us)
Async XLA Ops:
  0.0 1.0 %copy-start = (f32[1,2,8,64,128]{4,3,2,1,0:T(8,128)S(1)}, f32[1,2,8,64,128]{4,3,2,1,0:T(8,128)}, u32[]{:S(2)}) copy-start(f32[1,2,8,64,128]{4,3,2,1,0:T(8,128)} %start.3) | copy-start | bytes 1572868
  1.0 0.9 %copy-start.1 = (f32[8,64,128]{2,1,0:T(8,128)S(1)}, f32[8,64,128]{2,1,0:T(8,128)}, u32[]{:S(2)}) copy-start(f32[8,64,128]{2,1,0:T(8,128)} %conduct.3) | copy-start | bytes 786436
  2.0 0.9 %copy-start.2 = (f32[8,64,128]{2,1,0:T(8,128)S(1)}, f32[8,64,128]{2,1,0:T(8,128)}, u32[]{:S(2)}) copy-start(f32[8,64,128]{2,1,0:T(8,128)} %threshold.3) | copy-start | bytes 786436
  2.9 0.9 %copy-start.3 = (f32[8,64,128]{2,1,0:T(8,128)S(1)}, f32[8,64,128]{2,1,0:T(8,128)}, u32[]{:S(2)}) copy-start(f32[8,64,128]{2,1,0:T(8,128)} %recovery.3) | copy-start | bytes 786436
  5.7 9.5 %collective-permute-start = (f32[20,64,128]{2,1,0:T(8,128)S(1)}, f32[20,64,128]{2,1,0:T(8,128)S(1)}, u32[]{:S(2)}, u32[]{:S(2)}) collective-permute-start(f32[20,64,128]{2,1,0:T(8,128)S(1)} %get-tuple-element.34), channel_id=1, source_target_pairs={{0,1},{1,0},{2,3},{3,2},{4,5},{5,4},{6,7},{7,6},{8,9},{9,8},{10,11... | collective-permute-start | bytes 1966088 | tf_op jit(solution)/shard_map/ppermute | solution.py:434
  6.4 18.1 %collective-permute-start.1 = (f32[20,64,128]{2,1,0:T(8,128)S(1)}, f32[20,64,128]{2,1,0:T(8,128)S(1)}, u32[]{:S(2)}, u32[]{:S(2)}) collective-permute-start(f32[20,64,128]{2,1,0:T(8,128)S(1)} %get-tuple-element.35), channel_id=1, source_target_pairs={{1,2},{2,1},{5,6},{6,5},{9,10},{10,9},{13,14},{14,13},{17,18},{18,... | collective-permute-start | bytes 1966088 | tf_op jit(solution)/shard_map/ppermute | solution.py:435
  31.4 0.8 copy-start.8
  34.6 24.0 %copy-start.16 = (f32[6,64,128]{2,1,0:T(8,128)}, f32[6,64,128]{2,1,0:T(8,128)S(1)}, u32[]{:S(2)}) copy-start(f32[6,64,128]{2,1,0:T(8,128)S(1)} %get-tuple-element.52.d1r) | copy-start | bytes 589828
  34.6 24.0 %copy-start.18 = (f32[4,64,128]{2,1,0:T(8,128)}, f32[4,64,128]{2,1,0:T(8,128)S(1)}, u32[]{:S(2)}) copy-start(f32[4,64,128]{2,1,0:T(8,128)S(1)} %get-tuple-element.54.dlr) | copy-start | bytes 393220
  34.6 23.3 %collective-permute-start.2 = (f32[2,8,64,128]{3,2,1,0:T(8,128)S(1)}, f32[2,8,64,128]{3,2,1,0:T(8,128)S(1)}, u32[]{:S(2)}, u32[]{:S(2)}) collective-permute-start(f32[2,8,64,128]{3,2,1,0:T(8,128)S(1)} %get-tuple-element.36), channel_id=1, source_target_pairs={{0,4},{4,8},{8,12},{12,16},{16,20},{20,24},{24,28},{28,32},{32,36}... | collective-permute-start | bytes 1572872 | tf_op jit(solution)/shard_map/ppermute | solution.py:460
  37.8 42.3 %collective-permute-start.4 = (f32[5,64,128]{2,1,0:T(8,128)}, f32[5,64,128]{2,1,0:T(8,128)}, u32[]{:S(2)}, u32[]{:S(2)}) collective-permute-start(f32[5,64,128]{2,1,0:T(8,128)} %get-tuple-element.37), channel_id=1, source_target_pairs={{1,6},{2,5},{5,10},{6,9},{9,14},{10,13},{13,18},{14,17},{17,22},{1... | collective-permute-start | bytes 491528 | tf_op jit(solution)/shard_map/ppermute | solution.py:461
  58.6 21.5 %collective-permute-start.3 = (f32[5,64,128]{2,1,0:T(8,128)}, f32[5,64,128]{2,1,0:T(8,128)}, u32[]{:S(2)}, u32[]{:S(2)}) collective-permute-start(f32[5,64,128]{2,1,0:T(8,128)} %shard_map.48), channel_id=1, source_target_pairs={{0,1},{1,0},{2,3},{3,2},{4,5},{5,4},{6,7},{7,6},{8,9},{9,8},{10,11... | collective-permute-start | bytes 491528 | tf_op jit(solution)/shard_map/ppermute | solution.py:434
  58.6 8.5 %collective-permute-start.5 = (f32[4,32,128]{2,1,0:T(8,128)}, f32[4,32,128]{2,1,0:T(8,128)}, u32[]{:S(2)}, u32[]{:S(2)}) collective-permute-start(f32[4,32,128]{2,1,0:T(8,128)} %get-tuple-element.43), channel_id=1, source_target_pairs={{0,1},{1,0},{2,3},{3,2},{4,5},{5,4},{6,7},{7,6},{8,9},{9,8},{10,11... | collective-permute-start | bytes 196616 | tf_op jit(solution)/shard_map/ppermute | solution.py:434
  59.1 10.3 %collective-permute-start.6 = (f32[4,32,128]{2,1,0:T(8,128)}, f32[4,32,128]{2,1,0:T(8,128)}, u32[]{:S(2)}, u32[]{:S(2)}) collective-permute-start(f32[4,32,128]{2,1,0:T(8,128)} %get-tuple-element.44), channel_id=1, source_target_pairs={{1,2},{2,1},{5,6},{6,5},{9,10},{10,9},{13,14},{14,13},{17,18},{18,... | collective-permute-start | bytes 196616 | tf_op jit(solution)/shard_map/ppermute | solution.py:435
  69.4 1.0 %copy-start.5 = (f32[16,64,128]{2,1,0:T(8,128)S(1)}, f32[16,64,128]{2,1,0:T(8,128)}, u32[]{:S(2)}) copy-start(f32[16,64,128]{2,1,0:T(8,128)} %copy-done.4) | copy-start | bytes 1572868
  70.4 1.0 %copy-start.7 = (f32[16,64,128]{2,1,0:T(8,128)S(1)}, f32[16,64,128]{2,1,0:T(8,128)}, u32[]{:S(2)}) copy-start(f32[16,64,128]{2,1,0:T(8,128)} %copy-done.6) | copy-start | bytes 1572868
  71.5 1.0 %copy-start.9 = (f32[16,64,128]{2,1,0:T(8,128)S(1)}, f32[16,64,128]{2,1,0:T(8,128)}, u32[]{:S(2)}) copy-start(f32[16,64,128]{2,1,0:T(8,128)} %copy-done.8) | copy-start | bytes 1572868
  72.5 1.0 %copy-start.11 = (f32[16,64,128]{2,1,0:T(8,128)S(1)}, f32[16,64,128]{2,1,0:T(8,128)}, u32[]{:S(2)}) copy-start(f32[16,64,128]{2,1,0:T(8,128)} %copy-done.10) | copy-start | bytes 1572868
  73.6 1.0 %copy-start.13 = (f32[14,64,128]{2,1,0:T(8,128)S(1)}, f32[14,64,128]{2,1,0:T(8,128)}, u32[]{:S(2)}) copy-start(f32[14,64,128]{2,1,0:T(8,128)} %copy-done.12) | copy-start | bytes 1376260
  74.6 1.0 %copy-start.15 = (f32[14,64,128]{2,1,0:T(8,128)S(1)}, f32[14,64,128]{2,1,0:T(8,128)}, u32[]{:S(2)}) copy-start(f32[14,64,128]{2,1,0:T(8,128)} %copy-done.14) | copy-start | bytes 1376260
  75.6 0.9 copy-start.17
  76.5 0.9 copy-start.19
  85.1 7.6 %collective-permute-start.7 = (f32[1,32,128]{2,1,0:T(8,128)S(1)}, f32[1,32,128]{2,1,0:T(8,128)S(1)}, u32[]{:S(2)}, u32[]{:S(2)}) collective-permute-start(f32[1,32,128]{2,1,0:T(8,128)S(1)} %get-tuple-element.61), channel_id=1, source_target_pairs={{0,1},{1,0},{2,3},{3,2},{4,5},{5,4},{6,7},{7,6},{8,9},{9,8},{10,11... | collective-permute-start | bytes 49160 | tf_op jit(solution)/shard_map/ppermute | solution.py:434
  85.1 9.0 %collective-permute-start.8 = (f32[1,32,128]{2,1,0:T(8,128)S(1)}, f32[1,32,128]{2,1,0:T(8,128)S(1)}, u32[]{:S(2)}, u32[]{:S(2)}) collective-permute-start(f32[1,32,128]{2,1,0:T(8,128)S(1)} %get-tuple-element.62), channel_id=1, source_target_pairs={{1,2},{2,1},{5,6},{6,5},{9,10},{10,9},{13,14},{14,13},{17,18},{18,... | collective-permute-start | bytes 49160 | tf_op jit(solution)/shard_map/ppermute | solution.py:435
  (5 other events, 3.9 us)
